TPU v7x, 256 devices: a whole 4x4x8 slice. The times are simulated.
256 devices in a mesh: leaf: 16 (over y, x), col: 16 (over z, core).
Axes of the slice: x: 4, y: 4, z: 8, core: 2. Of those that a mesh axis runs over, the one named last changes fastest.
Arguments:
- right_sides: bfloat16 [16, 2, 1792, 128], P('leaf', None, 'col'), may hold values from -6 to 6
- leaf_inverse: bfloat16 [16, 1792, 1792], P('leaf', 'col'), as said below
- upper_inverse: bfloat16 [16, 1792, 1792], P('leaf', 'col'), as said below
- leaf_update: bfloat16 [16, 4, 1792, 512], P('leaf', None, 'col'), may hold values from -0.0625 to 0.0625
- upper_update: bfloat16 [16, 4, 1792, 512], P('leaf', None, 'col'), may hold values from -0.0625 to 0.0625
- live_rows: int32 [16, 2], P('leaf'), may hold values from 896 to 1792, as said below
- tile_map: int32 [16, 2, 4, 512], P('leaf'), may hold values from 0 to 1791, as said below
Outputs:
- solution: bfloat16 [16, 2, 1792, 128], P('leaf', None, 'col')
Inputs may be any that keep to these rules, and one draw needn't show every extreme that they name: `leaf_inverse`: zero above the diagonal, nonzero on it. `upper_inverse`: zero above the diagonal, nonzero on it. `live_rows`: one supernode has all 1792 rows live and one has 896. `tile_map`: the rows of one tile are distinct and increasing.
All inputs are finite; a program needn't handle non-finite values.
Results may differ from a plain program's by a relative error of at most 0.0075.
Values may be sent and summed in bfloat16 or wider, within the bound.
No kernel may reach another device: no remote copies, remote signals or barrier semaphores. Data moves between devices by JAX's collectives and lax.ppermute only.
A program may use at most 64 MiB of HBM per device.

v0:
```python
import jax
import jax.numpy as jnp
from jax import lax
from jax.sharding import PartitionSpec as P


def forward_solve(inverse_rows, residual, row_mask, active):
    shares = (residual * row_mask).astype(jnp.bfloat16)
    empty = jnp.zeros((inverse_rows.shape[0], residual.shape[1]), jnp.float32)
    shard_rows = lax.all_gather(shares, "col", axis=0, tiled=True)
    solved = lax.cond(
        active,
        lambda: jnp.dot(inverse_rows, shard_rows, preferred_element_type=jnp.float32),
        lambda: empty,
    )
    return (solved * row_mask).astype(jnp.bfloat16)


def tile_terms(update_cols, solved, active):

    def tile_compute():
        return jnp.einsum("srt,rn->stn", update_cols, solved, preferred_element_type=jnp.float32)

    def tile_nothing():
        return jnp.zeros((update_cols.shape[0], update_cols.shape[2], solved.shape[1]), jnp.float32)

    local_terms = lax.cond(active, tile_compute, tile_nothing)
    return lax.psum(local_terms, "col")


def spread(summed, tile_rows, first_row, rows_dev):
    local_rows = tile_rows - first_row
    inside = (local_rows >= 0) & (local_rows < rows_dev)
    target = jnp.where(inside, local_rows, rows_dev)

    def one_slot(values, where_to):
        return (
            jnp.zeros((rows_dev, values.shape[1]), jnp.float32)
            .at[where_to]
            .add(values, mode="drop")
        )

    return jax.vmap(one_slot)(summed, target)


def pick_rows(fetched, tile_rows, first_row, rows_dev):
    local_rows = tile_rows - first_row
    inside = (local_rows >= 0) & (local_rows < rows_dev)
    chosen = fetched[jnp.clip(local_rows, 0, rows_dev - 1)]
    return jnp.where(inside[:, None], chosen, jnp.zeros_like(chosen))


def backward_solve(inverse_rows, solved, pulled, row_mask, active):
    scaled = ((solved.astype(jnp.float32) - pulled) * row_mask).astype(jnp.bfloat16)
    rhs_width = scaled.shape[1]
    row_count = inverse_rows.shape[0] * lax.axis_size("col")

    def rows_compute():
        return lax.dot_general(
            inverse_rows, scaled, (((0,), (0,)), ((), ())), preferred_element_type=jnp.float32
        )

    summed = lax.psum_scatter(
        lax.cond(active, rows_compute, lambda: jnp.zeros((row_count, rhs_width), jnp.float32)),
        "col",
        scatter_dimension=0,
        tiled=True,
    )
    return (summed * row_mask).astype(jnp.bfloat16)


def pull_terms(update_cols, tiles, active):

    def pull_compute():
        return jnp.einsum("srt,stn->rn", update_cols, tiles, preferred_element_type=jnp.float32)

    def pull_nothing():
        return jnp.zeros((update_cols.shape[1], tiles.shape[2]), jnp.float32)

    return lax.cond(active, pull_compute, pull_nothing)


def deliver(outgoing, height, leaf_id, leaf_count):
    owner = leaf_id // 2**height * 2**height + 2 ** (height - 1)
    onehot = (jnp.arange(leaf_count, dtype=jnp.int32) == owner).astype(jnp.float32)
    slot_table = onehot[:, None, None] * outgoing[None]
    return lax.psum_scatter(slot_table, "leaf", scatter_dimension=0, tiled=True)[0]


def fetch(answer_up, height, leaf_id):
    owner = leaf_id // 2**height * 2**height + 2 ** (height - 1)
    gathered = lax.all_gather(answer_up[None], "leaf", axis=0, tiled=True)
    return lax.dynamic_index_in_dim(gathered, owner, 0, keepdims=False)


def shards(
    right_sides, leaf_inverse, upper_inverse, leaf_update, upper_update, live_rows, tile_map
):
    leaf_count = lax.axis_size("leaf")
    depth = leaf_count.bit_length() - 1
    rows_dev = leaf_inverse.shape[1]
    rhs_width = right_sides.shape[3]
    tile_len = tile_map.shape[3]
    leaf_id = lax.axis_index("leaf")
    col_id = lax.axis_index("col")
    first_row = col_id * rows_dev
    row_ids = first_row + jnp.arange(rows_dev, dtype=jnp.int32)
    leaf_mask = (row_ids < live_rows[0, 0]).astype(jnp.float32)[:, None]
    upper_mask = (row_ids < live_rows[0, 1]).astype(jnp.float32)[:, None]
    node_level = jnp.zeros((), jnp.int32)
    for height in range(1, depth + 1):
        node_level = node_level + ((leaf_id % 2 ** (height - 1) == 0) & (leaf_id > 0)).astype(
            jnp.int32
        )
    always = jnp.array(True)
    solved_leaf = forward_solve(
        leaf_inverse[0], right_sides[0, 0].astype(jnp.float32), leaf_mask, always
    )
    summed = tile_terms(leaf_update[0, :depth], solved_leaf, always)
    pieces = spread(summed, tile_map[0, 0, :depth], first_row, rows_dev)
    outgoing = [None] + [pieces[height - 1] for height in range(1, depth + 1)]
    residual_up = right_sides[0, 1].astype(jnp.float32)
    solved_up = jnp.zeros((rows_dev, rhs_width), jnp.bfloat16)
    for height in range(1, depth + 1):
        residual_up = residual_up - deliver(outgoing[height], height, leaf_id, leaf_count)
        active = node_level == height
        solved = forward_solve(upper_inverse[0], residual_up, upper_mask, active)
        solved_up = jnp.where(active, solved, solved_up)
        slot_count = depth - height
        if slot_count > 0:
            summed = tile_terms(upper_update[0, :slot_count], solved, active)
            pieces = spread(summed, tile_map[0, 1, :slot_count], first_row, rows_dev)
            for slot_idx in range(slot_count):
                outgoing[height + 1 + slot_idx] = outgoing[height + 1 + slot_idx] + pieces[slot_idx]
    answer_up = jnp.zeros((rows_dev, rhs_width), jnp.bfloat16)
    tiles_leaf = [None] * depth
    tiles_upper = jnp.zeros((depth, tile_len, rhs_width), jnp.bfloat16)
    for height in range(depth, 0, -1):
        active = node_level == height
        slot_count = depth - height
        if slot_count > 0:
            pulled = pull_terms(upper_update[0, :slot_count], tiles_upper[:slot_count], active)
        else:
            pulled = jnp.zeros((rows_dev, rhs_width), jnp.float32)
        answer = backward_solve(upper_inverse[0], solved_up, pulled, upper_mask, active)
        answer_up = jnp.where(active, answer, answer_up)
        fetched = fetch(answer_up, height, leaf_id)
        slot_now = jnp.clip(height - node_level - 1, 0, depth - 1)
        valid = (node_level > 0) & (node_level < height)
        upper_map = lax.dynamic_index_in_dim(tile_map[0, 1], slot_now, 0, keepdims=False)
        leaf_part = pick_rows(fetched, tile_map[0, 0, height - 1], first_row, rows_dev)
        upper_part = pick_rows(fetched, upper_map, first_row, rows_dev)
        upper_part = jnp.where(valid, upper_part, jnp.zeros_like(upper_part))
        both = (
            lax.psum(jnp.stack([leaf_part, upper_part]), "col")
            .astype(jnp.float32)
            .astype(jnp.bfloat16)
        )
        tiles_leaf[height - 1] = both[0]
        updated = lax.dynamic_update_index_in_dim(tiles_upper, both[1], slot_now, 0)
        tiles_upper = jnp.where(valid, updated, tiles_upper)
    pulled = pull_terms(leaf_update[0, :depth], jnp.stack(tiles_leaf), always)
    answer_leaf = backward_solve(leaf_inverse[0], solved_leaf, pulled, leaf_mask, always)
    return jnp.stack([answer_leaf, answer_up])[None]


def solution(mesh):
    placed = (
        P("leaf", None, "col", None),
        P("leaf", "col", None),
        P("leaf", "col", None),
        P("leaf", None, "col", None),
        P("leaf", None, "col", None),
        P("leaf", None),
        P("leaf", None, None, None),
    )
    return jax.shard_map(
        shards, mesh=mesh, in_specs=placed, out_specs=P("leaf", None, "col", None), check_vma=False
    )
```

profile of v0, /device:TPU:4, one launch (start us, length us, event | category | flops | bytes accessed | tf_op | source)
XLA Modules:
  0.0 1755.9 jit_solution(690837087671866343)
XLA Ops:
  9.4 21.2 %all_gather.27 = bf16[1792,128]{1,0:T(8,128)(2,1)S(1)} all-gather(bf16[112,128]{1,0:T(8,128)(2,1)S(1)} %fusion.53), channel_id=1, replica_groups=mesh['leaf'=16,'col'=16] {'col'}, dimensions={0}, use_global_device_ids=true | all-gather | bytes 487424 | tf_op jit(solution)/shard_map/all_gather | solution.py:10
  34.5 108.2 %all-reduce.13.cloned.1.call-done = f32[4,512,128]{1,2,0:T(8,128)} async-done(((f32[4,512,128]{1,2,0:T(8,128)}), f32[4,512,128]{1,2,0:T(8,128)}) %all-reduce.13.cloned.1.call-update) | async-done | bytes 1048592 | tf_op jit(solution)/shard_map/psum | solution.py:28
  158.6 77.5 %reduce-scatter.38.cloned.1.call-done = f32[1,112,128]{2,1,0:T(8,128)} async-done(((f32[16,112,128]{2,1,0:T(8,128)}), f32[1,112,128]{2,1,0:T(8,128)}) %reduce-scatter.38.cloned.1.call-update) | async-done | bytes 57360
  257.0 109.0 %all-reduce.15.cloned.1.call-done = f32[3,512,128]{2,1,0:T(8,128)} async-done(((f32[3,512,128]{2,1,0:T(8,128)}), f32[3,512,128]{2,1,0:T(8,128)}) %all-reduce.15.cloned.1.call-update) | async-done | bytes 786448 | tf_op jit(solution)/shard_map/psum | solution.py:28
  377.1 78.3 %reduce-scatter.40.cloned.1.call-done = f32[1,112,128]{2,1,0:T(8,128)} async-done(((f32[16,112,128]{2,1,0:T(8,128)}), f32[1,112,128]{2,1,0:T(8,128)}) %reduce-scatter.40.cloned.1.call-update) | async-done | bytes 57360
  456.3 18.7 %all_gather.29 = bf16[1792,128]{1,0:T(8,128)(2,1)S(1)} all-gather(bf16[112,128]{1,0:T(8,128)(2,1)S(1)} %get-tuple-element.234), channel_id=1, replica_groups=mesh['leaf'=16,'col'=16] {'col'}, dimensions={0}, use_global_device_ids=true | all-gather | bytes 487424 | tf_op jit(solution)/shard_map/all_gather | solution.py:10
  476.6 107.9 %all-reduce.17.cloned.1.call-done = f32[2,512,128]{2,1,0:T(8,128)} async-done(((f32[2,512,128]{2,1,0:T(8,128)}), f32[2,512,128]{2,1,0:T(8,128)}) %all-reduce.17.cloned.1.call-update) | async-done | bytes 524304 | tf_op jit(solution)/shard_map/psum | solution.py:28
  592.1 79.1 %reduce-scatter.42.cloned.1.call-done = f32[1,112,128]{2,1,0:T(8,128)} async-done(((f32[16,112,128]{2,1,0:T(8,128)}), f32[1,112,128]{2,1,0:T(8,128)}) %reduce-scatter.42.cloned.1.call-update) | async-done | bytes 57360
  672.2 18.7 %all_gather.30 = bf16[1792,128]{1,0:T(8,128)(2,1)S(1)} all-gather(bf16[112,128]{1,0:T(8,128)(2,1)S(1)} %multiply_convert_fusion.7), channel_id=1, replica_groups=mesh['leaf'=16,'col'=16] {'col'}, dimensions={0}, use_global_device_ids=true | all-gather | bytes 487424 | tf_op jit(solution)/shard_map/all_gather | solution.py:10
  691.8 106.9 %all-reduce.19.cloned.1.call-done = f32[1,512,128]{2,1,0:T(8,128)} async-done(((f32[1,512,128]{2,1,0:T(8,128)}), f32[1,512,128]{2,1,0:T(8,128)}) %all-reduce.19.cloned.1.call-update) | async-done | bytes 262160 | tf_op jit(solution)/shard_map/psum | solution.py:28
  803.8 79.3 %reduce-scatter.44.cloned.1.call-done = f32[1,112,128]{2,1,0:T(8,128)} async-done(((f32[16,112,128]{2,1,0:T(8,128)}), f32[1,112,128]{2,1,0:T(8,128)}) %reduce-scatter.44.cloned.1.call-update) | async-done | bytes 57360
  906.3 52.8 %reduce-scatter.28.cloned.1.call-done = f32[112,128]{1,0:T(8,128)} async-done(((f32[1792,128]{1,0:T(8,128)}), f32[112,128]{1,0:T(8,128)}) %reduce-scatter.28.cloned.1.call-update) | async-done | bytes 57360 | tf_op jit(solution)/shard_map/reduce_scatter | solution.py:63
  960.0 23.5 %all-gather = bf16[1792,128]{1,0:T(8,128)(2,1)S(1)} all-gather(bf16[112,128]{1,0:T(8,128)(2,1)S(1)} %fusion.60), channel_id=2, replica_groups=mesh['leaf'=16,'col'=16] {'leaf'}, dimensions={0}, use_global_device_ids=true | all-gather | bytes 487424 | tf_op jit(solution)/shard_map/all_gather | solution.py:92
  987.3 107.1 %all-reduce.21.cloned.1.call-done = bf16[2,512,128]{2,1,0:T(8,128)(2,1)} async-done(((bf16[2,512,128]{2,1,0:T(8,128)(2,1)}), bf16[2,512,128]{2,1,0:T(8,128)(2,1)}) %all-reduce.21.cloned.1.call-update) | async-done | bytes 262160 | tf_op jit(solution)/shard_map/psum | solution.py:155
  1096.6 58.6 %reduce-scatter.30.cloned.1.call-done = f32[112,128]{1,0:T(8,128)} async-done(((f32[1792,128]{1,0:T(8,128)}), f32[112,128]{1,0:T(8,128)}) %reduce-scatter.30.cloned.1.call-update) | async-done | bytes 57360 | tf_op jit(solution)/shard_map/reduce_scatter | solution.py:63
  1156.2 23.6 %all-gather.1 = bf16[1792,128]{1,0:T(8,128)(2,1)S(1)} all-gather(bf16[112,128]{1,0:T(8,128)(2,1)S(1)} %fusion.61), channel_id=3, replica_groups=mesh['leaf'=16,'col'=16] {'leaf'}, dimensions={0}, use_global_device_ids=true | all-gather | bytes 487424 | tf_op jit(solution)/shard_map/all_gather | solution.py:92
  1183.5 107.0 %all-reduce.23.cloned.1.call-done = bf16[2,512,128]{2,1,0:T(8,128)(2,1)} async-done(((bf16[2,512,128]{2,1,0:T(8,128)(2,1)}), bf16[2,512,128]{2,1,0:T(8,128)(2,1)}) %all-reduce.23.cloned.1.call-update) | async-done | bytes 262160 | tf_op jit(solution)/shard_map/psum | solution.py:155
  1293.9 58.4 %reduce-scatter.32.cloned.1.call-done = f32[112,128]{1,0:T(8,128)} async-done(((f32[1792,128]{1,0:T(8,128)}), f32[112,128]{1,0:T(8,128)}) %reduce-scatter.32.cloned.1.call-update) | async-done | bytes 57360 | tf_op jit(solution)/shard_map/reduce_scatter | solution.py:63
  1353.1 23.6 %all-gather.2 = bf16[1792,128]{1,0:T(8,128)(2,1)S(1)} all-gather(bf16[112,128]{1,0:T(8,128)(2,1)S(1)} %fusion.62), channel_id=4, replica_groups=mesh['leaf'=16,'col'=16] {'leaf'}, dimensions={0}, use_global_device_ids=true | all-gather | bytes 487424 | tf_op jit(solution)/shard_map/all_gather | solution.py:92
  1381.7 107.2 %all-reduce.25.cloned.1.call-done = bf16[2,512,128]{2,1,0:T(8,128)(2,1)} async-done(((bf16[2,512,128]{2,1,0:T(8,128)(2,1)}), bf16[2,512,128]{2,1,0:T(8,128)(2,1)}) %all-reduce.25.cloned.1.call-update) | async-done | bytes 262160 | tf_op jit(solution)/shard_map/psum | solution.py:155
  1491.0 58.9 %reduce-scatter.34.cloned.1.call-done = f32[112,128]{1,0:T(8,128)} async-done(((f32[1792,128]{1,0:T(8,128)}), f32[112,128]{1,0:T(8,128)}) %reduce-scatter.34.cloned.1.call-update) | async-done | bytes 57360 | tf_op jit(solution)/shard_map/reduce_scatter | solution.py:63
  1550.7 23.6 %all-gather.3 = bf16[1792,128]{1,0:T(8,128)(2,1)S(1)} all-gather(bf16[112,128]{1,0:T(8,128)(2,1)S(1)} %fusion.63), channel_id=5, replica_groups=mesh['leaf'=16,'col'=16] {'leaf'}, dimensions={0}, use_global_device_ids=true | all-gather | bytes 487424 | tf_op jit(solution)/shard_map/all_gather | solution.py:92
  1580.2 106.1 %all-reduce.27.cloned.1.call-done = bf16[2,512,128]{2,1,0:T(8,128)(2,1)} async-done(((bf16[2,512,128]{2,1,0:T(8,128)(2,1)}), bf16[2,512,128]{2,1,0:T(8,128)(2,1)}) %all-reduce.27.cloned.1.call-update) | async-done | bytes 262160 | tf_op jit(solution)/shard_map/psum | solution.py:155
  1689.1 58.7 %reduce-scatter.36.cloned.1.call-done = f32[112,128]{1,0:T(8,128)} async-done(((f32[1792,128]{1,0:T(8,128)}), f32[112,128]{1,0:T(8,128)}) %reduce-scatter.36.cloned.1.call-update) | async-done | bytes 57360 | tf_op jit(solution)/shard_map/reduce_scatter | solution.py:63
  (241 shorter events, 128.8 us)
Async XLA Ops:
  6.5 136.2 %all-reduce.13.cloned.1.call-start = ((), (), s32[]{:S(2)}) async-start(), calls=%async_computation.9 | async-start | bytes 2097152 | tf_op jit(solution)/shard_map/psum | solution.py:28
  32.3 203.8 %reduce-scatter.38.cloned.1.call-start = ((), (), s32[]{:S(2)}) async-start(), calls=%async_computation.22 | async-start | bytes 974848
  156.9 209.0 %all-reduce.15.cloned.1.call-start = ((), (), s32[]{:S(2)}) async-start(), calls=%async_computation.10 | async-start | bytes 1572864 | tf_op jit(solution)/shard_map/psum | solution.py:28
  158.5 77.6 %copy-start.24 = (bf16[1,2,112,128]{3,2,1,0:T(8,128)(2,1)S(1)}, bf16[1,2,112,128]{3,2,1,0:T(8,128)(2,1)}, u32[]{:S(2)}) copy-start(bf16[1,2,112,128]{3,2,1,0:T(8,128)(2,1)} %param.35) | copy-start | bytes 172036
  158.6 97.1 %copy-start.1 = (bf16[1,112,1792]{2,1,0:T(8,128)(2,1)S(1)}, bf16[1,112,1792]{2,1,0:T(8,128)(2,1)}, u32[]{:S(2)}) copy-start(bf16[1,112,1792]{2,1,0:T(8,128)(2,1)} %param.37) | copy-start | bytes 1204228
  256.8 198.6 %reduce-scatter.40.cloned.1.call-start = ((), (), s32[]{:S(2)}) async-start(), calls=%async_computation.23 | async-start | bytes 974848
  376.2 208.2 %all-reduce.17.cloned.1.call-start = ((), (), s32[]{:S(2)}) async-start(), calls=%async_computation.11 | async-start | bytes 1048576 | tf_op jit(solution)/shard_map/psum | solution.py:28
  377.1 78.4 %copy-start.20 = (f32[1,112,128]{2,1,0:T(8,128)S(1)}, f32[1,112,128]{2,1,0:T(8,128)}, u32[]{:S(2)}) copy-start(f32[1,112,128]{2,1,0:T(8,128)} %reduce-scatter.38.cloned.1.call-done) | copy-start | bytes 172036
  476.5 194.8 %reduce-scatter.42.cloned.1.call-start = ((), (), s32[]{:S(2)}) async-start(), calls=%async_computation.24 | async-start | bytes 974848
  592.0 206.7 %all-reduce.19.cloned.1.call-start = ((), (), s32[]{:S(2)}) async-start(), calls=%async_computation.12 | async-start | bytes 524288 | tf_op jit(solution)/shard_map/psum | solution.py:28
  691.7 191.4 %reduce-scatter.44.cloned.1.call-start = ((), (), s32[]{:S(2)}) async-start(), calls=%async_computation.25 | async-start | bytes 974848
  803.7 79.4 %copy-start.22 = (f32[1,112,128]{2,1,0:T(8,128)S(1)}, f32[1,112,128]{2,1,0:T(8,128)}, u32[]{:S(2)}) copy-start(f32[1,112,128]{2,1,0:T(8,128)} %reduce-scatter.42.cloned.1.call-done) | copy-start | bytes 172036
  803.7 155.4 %reduce-scatter.28.cloned.1.call-start = ((), (), s32[]{:S(2)}) async-start(), calls=%async_computation.17 | async-start | bytes 974848 | tf_op jit(solution)/shard_map/reduce_scatter | solution.py:63
  902.8 192.6 %copy-start.11 = (bf16[112,128]{1,0:T(8,128)(2,1)}, bf16[112,128]{1,0:T(8,128)(2,1)S(1)}, u32[]{:S(2)}) copy-start(bf16[112,128]{1,0:T(8,128)(2,1)S(1)} %get-tuple-element.233) | copy-start | bytes 86020
  903.8 190.5 %all-reduce.21.cloned.1.call-start = ((), (), s32[]{:S(2)}) async-start(), calls=%async_computation.13 | async-start | bytes 524288 | tf_op jit(solution)/shard_map/psum | solution.py:155
  987.2 168.0 %reduce-scatter.30.cloned.1.call-start = ((), (), s32[]{:S(2)}) async-start(), calls=%async_computation.18 | async-start | bytes 974848 | tf_op jit(solution)/shard_map/reduce_scatter | solution.py:63
  1095.6 59.7 %copy-start.21 = (f32[112,128]{1,0:T(8,128)S(1)}, f32[112,128]{1,0:T(8,128)}, u32[]{:S(2)}) copy-start(f32[112,128]{1,0:T(8,128)} %reduce-scatter.28.cloned.1.call-done) | copy-start | bytes 172036
  1096.5 194.1 %all-reduce.23.cloned.1.call-start = ((), (), s32[]{:S(2)}) async-start(), calls=%async_computation.14 | async-start | bytes 524288 | tf_op jit(solution)/shard_map/psum | solution.py:155
  1183.5 168.7 %reduce-scatter.32.cloned.1.call-start = ((), (), s32[]{:S(2)}) async-start(), calls=%async_computation.19 | async-start | bytes 974848 | tf_op jit(solution)/shard_map/reduce_scatter | solution.py:63
  1293.8 195.2 %all-reduce.25.cloned.1.call-start = ((), (), s32[]{:S(2)}) async-start(), calls=%async_computation.15 | async-start | bytes 524288 | tf_op jit(solution)/shard_map/psum | solution.py:155
  1381.7 168.1 %reduce-scatter.34.cloned.1.call-start = ((), (), s32[]{:S(2)}) async-start(), calls=%async_computation.20 | async-start | bytes 974848 | tf_op jit(solution)/shard_map/reduce_scatter | solution.py:63
  1490.9 195.5 %all-reduce.27.cloned.1.call-start = ((), (), s32[]{:S(2)}) async-start(), calls=%async_computation.16 | async-start | bytes 524288 | tf_op jit(solution)/shard_map/psum | solution.py:155
  1579.3 168.5 %reduce-scatter.36.cloned.1.call-start = ((), (), s32[]{:S(2)}) async-start(), calls=%async_computation.21 | async-start | bytes 974848 | tf_op jit(solution)/shard_map/reduce_scatter | solution.py:63
  1580.2 106.1 %copy-start.17 = (bf16[128,112]{0,1:T(8,128)(2,1)S(1)}, bf16[128,112]{0,1:T(8,128)(2,1)}, u32[]{:S(2)}) copy-start(bf16[128,112]{0,1:T(8,128)(2,1)} %copy-done.16) | copy-start | bytes 86020
  (29 other events, 152.0 us)
Sparse Core Ops, SparseCore 0:
  32.4 110.2 all-reduce.12
  157.1 78.9 reduce-scatter.37
  256.9 108.9 all-reduce.14
  376.3 79.0 reduce-scatter.39
  476.6 107.7 all-reduce.16
  592.1 79.0 reduce-scatter.41
  691.8 106.8 all-reduce.18
  803.8 79.1 reduce-scatter.43
  903.9 55.1 reduce-scatter.27
  987.3 106.9 all-reduce.20
  1096.9 58.3 reduce-scatter.29
  1183.6 106.9 all-reduce.22
  1293.9 58.3 reduce-scatter.31
  1381.8 107.1 all-reduce.24
  1491.3 58.4 reduce-scatter.33
  1579.4 106.9 all-reduce.26
  1689.2 58.5 reduce-scatter.35
where the time goes:
time: 1760 us
  waiting for transfers between devices  1460 us (83%)
  blocking collectives  190 us (11%)
  other arithmetic  54.8 us (3%)
  local copies, waits for them, and re-layouts  31.1 us (2%)
    psum x4, waiting for transfers between devices, tile_terms(): return lax.psum(local_terms, 'col')  432 us
    psum x4, waiting for transfers between devices, shards(): lax.psum(jnp.stack([leaf_part, upper_part]), 'col').astype(jnp.float32)  427 us
    unnamed x21, waiting for transfers between devices  315 us
    reduce_scatter x5, waiting for transfers between devices, backward_solve(): lax.psum_scatter(lax.cond(active, rows_compute, lambda: jnp.zeros((row_co...  287 us
    all_gather x5, blocking collectives, forward_solve(): shard_rows = lax.all_gather(shares, 'col', axis=0, tiled=True)  96 us
    all_gather x4, blocking collectives, fetch(): gathered = lax.all_gather(answer_up[None], 'leaf', axis=0, tiled=True)  94.3 us
  transfers between devices with their start and end apart: 17, of which 17 were waited for; matrix products, arithmetic and copies ran while one was open for 0% of the time, Pallas kernels for 0%

commit v1 on v0

--- a/solution.py
+++ b/solution.py
@@ -2,6 +2,11 @@
 import jax.numpy as jnp
 from jax import lax
 from jax.sharding import PartitionSpec as P
+
+
+def _guide_region(inputs):
+    long_array = jnp.sum(jax.lax.all_gather(inputs, "col"), axis=0)
+    return long_array
 
 
 def forward_solve(inverse_rows, residual, row_mask, active):
@@ -25,7 +30,7 @@
         return jnp.zeros((update_cols.shape[0], update_cols.shape[2], solved.shape[1]), jnp.float32)
 
     local_terms = lax.cond(active, tile_compute, tile_nothing)
-    return lax.psum(local_terms, "col")
+    return _guide_region(local_terms)
 
 
 def spread(summed, tile_rows, first_row, rows_dev):

time: 1760 us -> 1590 us (0.903)
  waiting for transfers between devices: 1460 us -> 1280 us
  other arithmetic: 54.8 us -> 81.3 us
    psum x4 -> x0, waiting for transfers between devices: 432 us -> none  [tile_terms(): return lax.psum(local_terms, 'col')]
    all_gather x0 -> x4, waiting for transfers between devices: none -> 256 us  [_guide_region(): long_array = jnp.sum(jax.lax.all_gather(inputs, 'col'), axis=0)]
    reduce_sum x0 -> x4, other arithmetic: none -> 18.2 us  [_guide_region(): long_array = jnp.sum(jax.lax.all_gather(inputs, 'col'), axis=0)]
where the time goes in v1:
time: 1590 us
  waiting for transfers between devices  1280 us (81%)
  blocking collectives  190 us (12%)
  other arithmetic  81.3 us (5%)
  local copies, waits for them, and re-layouts  23.9 us (2%)
    psum x4, waiting for transfers between devices, shards(): lax.psum(jnp.stack([leaf_part, upper_part]), 'col').astype(jnp.float32)  427 us
    unnamed x21, waiting for transfers between devices  309 us
    reduce_scatter x5, waiting for transfers between devices, backward_solve(): lax.psum_scatter(lax.cond(active, rows_compute, lambda: jnp.zeros((row_co...  287 us
    all_gather x4, waiting for transfers between devices, _guide_region(): long_array = jnp.sum(jax.lax.all_gather(inputs, 'col'), axis=0)  256 us
    all_gather x5, blocking collectives, forward_solve(): shard_rows = lax.all_gather(shares, 'col', axis=0, tiled=True)  95.9 us
    all_gather x4, blocking collectives, fetch(): gathered = lax.all_gather(answer_up[None], 'leaf', axis=0, tiled=True)  94 us
  transfers between devices with their start and end apart: 17, of which 17 were waited for; matrix products, arithmetic and copies ran while one was open for 0% of the time, Pallas kernels for 0%

profile of v1, /device:TPU:4, one launch (start us, length us, event | category | flops | bytes accessed | tf_op | source)
XLA Modules:
  0.0 1592.5 jit_solution(1535010778906564018)
XLA Ops:
  9.4 21.2 %all_gather.51 = bf16[1792,128]{1,0:T(8,128)(2,1)S(1)} all-gather(bf16[112,128]{1,0:T(8,128)(2,1)S(1)} %fusion.51), channel_id=1, replica_groups=mesh['leaf'=16,'col'=16] {'col'}, dimensions={0}, use_global_device_ids=true | all-gather | bytes 487424 | tf_op jit(solution)/shard_map/all_gather | solution.py:15
  36.5 91.3 %all-gather.13.cloned.1.call-done = f32[64,512,128]{2,1,0:T(8,128)} async-done(((f32[4,512,128]{2,1,0:T(8,128)}), f32[64,512,128]{2,1,0:T(8,128)}) %all-gather.13.cloned.1.call-update) | async-done | bytes 16777232 | tf_op jit(solution)/shard_map/all_gather | solution.py:8
  147.9 76.6 %reduce-scatter.38.cloned.1.call-done = f32[1,112,128]{2,1,0:T(8,128)} async-done(((f32[16,112,128]{2,1,0:T(8,128)}), f32[1,112,128]{2,1,0:T(8,128)}) %reduce-scatter.38.cloned.1.call-update) | async-done | bytes 57360
  225.5 18.7 %all_gather.54 = bf16[1792,128]{1,0:T(8,128)(2,1)S(1)} all-gather(bf16[112,128]{1,0:T(8,128)(2,1)S(1)} %multiply_convert_fusion.11), channel_id=1, replica_groups=mesh['leaf'=16,'col'=16] {'col'}, dimensions={0}, use_global_device_ids=true | all-gather | bytes 487424 | tf_op jit(solution)/shard_map/all_gather | solution.py:15
  245.7 72.7 %all-gather.15.cloned.1.call-done = f32[48,512,128]{2,1,0:T(8,128)} async-done(((f32[3,512,128]{2,1,0:T(8,128)}), f32[48,512,128]{2,1,0:T(8,128)}) %all-gather.15.cloned.1.call-update) | async-done | bytes 12582928 | tf_op jit(solution)/shard_map/all_gather | solution.py:8
  333.7 77.3 %reduce-scatter.40.cloned.1.call-done = f32[1,112,128]{2,1,0:T(8,128)} async-done(((f32[16,112,128]{2,1,0:T(8,128)}), f32[1,112,128]{2,1,0:T(8,128)}) %reduce-scatter.40.cloned.1.call-update) | async-done | bytes 57360
  411.9 18.7 %all_gather.57 = bf16[1792,128]{1,0:T(8,128)(2,1)S(1)} all-gather(bf16[112,128]{1,0:T(8,128)(2,1)S(1)} %get-tuple-element.234), channel_id=1, replica_groups=mesh['leaf'=16,'col'=16] {'col'}, dimensions={0}, use_global_device_ids=true | all-gather | bytes 487424 | tf_op jit(solution)/shard_map/all_gather | solution.py:15
  432.4 52.8 %all-gather.17.cloned.1.call-done = f32[32,512,128]{2,1,0:T(8,128)} async-done(((f32[2,512,128]{2,1,0:T(8,128)}), f32[32,512,128]{2,1,0:T(8,128)}) %all-gather.17.cloned.1.call-update) | async-done | bytes 8388624 | tf_op jit(solution)/shard_map/all_gather | solution.py:8
  496.2 77.4 %reduce-scatter.42.cloned.1.call-done = f32[1,112,128]{2,1,0:T(8,128)} async-done(((f32[16,112,128]{2,1,0:T(8,128)}), f32[1,112,128]{2,1,0:T(8,128)}) %reduce-scatter.42.cloned.1.call-update) | async-done | bytes 57360
  594.4 38.8 %all-gather.19.cloned.1.call-done = f32[16,512,128]{2,1,0:T(8,128)} async-done(((f32[1,512,128]{2,1,0:T(8,128)}), f32[16,512,128]{2,1,0:T(8,128)}) %all-gather.19.cloned.1.call-update) | async-done | bytes 4194320 | tf_op jit(solution)/shard_map/all_gather | solution.py:8
  640.1 77.4 %reduce-scatter.44.cloned.1.call-done = f32[1,112,128]{2,1,0:T(8,128)} async-done(((f32[16,112,128]{2,1,0:T(8,128)}), f32[1,112,128]{2,1,0:T(8,128)}) %reduce-scatter.44.cloned.1.call-update) | async-done | bytes 57360
  740.7 52.7 %reduce-scatter.28.cloned.1.call-done = f32[112,128]{1,0:T(8,128)} async-done(((f32[1792,128]{1,0:T(8,128)}), f32[112,128]{1,0:T(8,128)}) %reduce-scatter.28.cloned.1.call-update) | async-done | bytes 57360 | tf_op jit(solution)/shard_map/reduce_scatter | solution.py:68
  794.3 23.5 %all-gather.4 = bf16[1792,128]{1,0:T(8,128)(2,1)S(1)} all-gather(bf16[112,128]{1,0:T(8,128)(2,1)S(1)} %fusion.58), channel_id=6, replica_groups=mesh['leaf'=16,'col'=16] {'leaf'}, dimensions={0}, use_global_device_ids=true | all-gather | bytes 487424 | tf_op jit(solution)/shard_map/all_gather | solution.py:97
  821.6 107.1 %all-reduce.9.cloned.1.call-done = bf16[2,512,128]{2,1,0:T(8,128)(2,1)} async-done(((bf16[2,512,128]{2,1,0:T(8,128)(2,1)}), bf16[2,512,128]{2,1,0:T(8,128)(2,1)}) %all-reduce.9.cloned.1.call-update) | async-done | bytes 262160 | tf_op jit(solution)/shard_map/psum | solution.py:160
  931.0 58.5 %reduce-scatter.30.cloned.1.call-done = f32[112,128]{1,0:T(8,128)} async-done(((f32[1792,128]{1,0:T(8,128)}), f32[112,128]{1,0:T(8,128)}) %reduce-scatter.30.cloned.1.call-update) | async-done | bytes 57360 | tf_op jit(solution)/shard_map/reduce_scatter | solution.py:68
  990.5 23.6 %all-gather.5 = bf16[1792,128]{1,0:T(8,128)(2,1)S(1)} all-gather(bf16[112,128]{1,0:T(8,128)(2,1)S(1)} %fusion.59), channel_id=7, replica_groups=mesh['leaf'=16,'col'=16] {'leaf'}, dimensions={0}, use_global_device_ids=true | all-gather | bytes 487424 | tf_op jit(solution)/shard_map/all_gather | solution.py:97
  1019.1 107.0 %all-reduce.11.cloned.1.call-done = bf16[2,512,128]{2,1,0:T(8,128)(2,1)} async-done(((bf16[2,512,128]{2,1,0:T(8,128)(2,1)}), bf16[2,512,128]{2,1,0:T(8,128)(2,1)}) %all-reduce.11.cloned.1.call-update) | async-done | bytes 262160 | tf_op jit(solution)/shard_map/psum | solution.py:160
  1130.9 57.3 %reduce-scatter.32.cloned.1.call-done = f32[112,128]{1,0:T(8,128)} async-done(((f32[1792,128]{1,0:T(8,128)}), f32[112,128]{1,0:T(8,128)}) %reduce-scatter.32.cloned.1.call-update) | async-done | bytes 57360 | tf_op jit(solution)/shard_map/reduce_scatter | solution.py:68
  1189.1 23.4 %all-gather.6 = bf16[1792,128]{1,0:T(8,128)(2,1)S(1)} all-gather(bf16[112,128]{1,0:T(8,128)(2,1)S(1)} %fusion.60), channel_id=8, replica_groups=mesh['leaf'=16,'col'=16] {'leaf'}, dimensions={0}, use_global_device_ids=true | all-gather | bytes 487424 | tf_op jit(solution)/shard_map/all_gather | solution.py:97
  1217.5 107.0 %all-reduce.13.cloned.1.call-done = bf16[2,512,128]{2,1,0:T(8,128)(2,1)} async-done(((bf16[2,512,128]{2,1,0:T(8,128)(2,1)}), bf16[2,512,128]{2,1,0:T(8,128)(2,1)}) %all-reduce.13.cloned.1.call-update) | async-done | bytes 262160 | tf_op jit(solution)/shard_map/psum | solution.py:160
  1326.5 59.6 %reduce-scatter.34.cloned.1.call-done = f32[112,128]{1,0:T(8,128)} async-done(((f32[1792,128]{1,0:T(8,128)}), f32[112,128]{1,0:T(8,128)}) %reduce-scatter.34.cloned.1.call-update) | async-done | bytes 57360 | tf_op jit(solution)/shard_map/reduce_scatter | solution.py:68
  1387.0 23.6 %all-gather.7 = bf16[1792,128]{1,0:T(8,128)(2,1)S(1)} all-gather(bf16[112,128]{1,0:T(8,128)(2,1)S(1)} %fusion.61), channel_id=9, replica_groups=mesh['leaf'=16,'col'=16] {'leaf'}, dimensions={0}, use_global_device_ids=true | all-gather | bytes 487424 | tf_op jit(solution)/shard_map/all_gather | solution.py:97
  1416.5 105.9 %all-reduce.15.cloned.1.call-done = bf16[2,512,128]{2,1,0:T(8,128)(2,1)} async-done(((bf16[2,512,128]{2,1,0:T(8,128)(2,1)}), bf16[2,512,128]{2,1,0:T(8,128)(2,1)}) %all-reduce.15.cloned.1.call-update) | async-done | bytes 262160 | tf_op jit(solution)/shard_map/psum | solution.py:160
  1526.0 58.5 %reduce-scatter.36.cloned.1.call-done = f32[112,128]{1,0:T(8,128)} async-done(((f32[1792,128]{1,0:T(8,128)}), f32[112,128]{1,0:T(8,128)}) %reduce-scatter.36.cloned.1.call-update) | async-done | bytes 57360 | tf_op jit(solution)/shard_map/reduce_scatter | solution.py:68
  (216 shorter events, 149.1 us)
Async XLA Ops:
  6.5 121.2 %all-gather.13.cloned.1.call-start = ((), (), s32[]{:S(2)}) async-start(), calls=%async_computation.13 | async-start | bytes 17825792 | tf_op jit(solution)/shard_map/all_gather | solution.py:8
  32.5 192.0 %copy-start.17 = (bf16[1,2,112,128]{3,2,1,0:T(8,128)(2,1)S(1)}, bf16[1,2,112,128]{3,2,1,0:T(8,128)(2,1)}, u32[]{:S(2)}) copy-start(bf16[1,2,112,128]{3,2,1,0:T(8,128)(2,1)} %param.35) | copy-start | bytes 172036
  32.8 211.4 %copy-start.1 = (bf16[1,112,1792]{2,1,0:T(8,128)(2,1)S(1)}, bf16[1,112,1792]{2,1,0:T(8,128)(2,1)}, u32[]{:S(2)}) copy-start(bf16[1,112,1792]{2,1,0:T(8,128)(2,1)} %param.37) | copy-start | bytes 1204228
  34.2 190.3 %reduce-scatter.38.cloned.1.call-start = ((), (), s32[]{:S(2)}) async-start(), calls=%async_computation.22 | async-start | bytes 974848
  147.1 285.1 %copy-start.20 = (s32[2]{0:T(128)S(1)}, s32[2]{0:T(128)}, u32[]{:S(2)}) copy-start(s32[2]{0:T(128)} %constant.231) | copy-start | bytes 28
  147.1 171.3 %all-gather.15.cloned.1.call-start = ((), (), s32[]{:S(2)}) async-start(), calls=%async_computation.14 | async-start | bytes 13369344 | tf_op jit(solution)/shard_map/all_gather | solution.py:8
  224.5 186.4 %copy-start.14 = (f32[1,112,128]{2,1,0:T(8,128)S(1)}, f32[1,112,128]{2,1,0:T(8,128)}, u32[]{:S(2)}) copy-start(f32[1,112,128]{2,1,0:T(8,128)} %reduce-scatter.38.cloned.1.call-done) | copy-start | bytes 172036
  245.4 165.6 %reduce-scatter.40.cloned.1.call-start = ((), (), s32[]{:S(2)}) async-start(), calls=%async_computation.23 | async-start | bytes 974848
  333.6 151.6 %all-gather.17.cloned.1.call-start = ((), (), s32[]{:S(2)}) async-start(), calls=%async_computation.15 | async-start | bytes 8912896 | tf_op jit(solution)/shard_map/all_gather | solution.py:8
  432.1 141.5 %reduce-scatter.42.cloned.1.call-start = ((), (), s32[]{:S(2)}) async-start(), calls=%async_computation.24 | async-start | bytes 974848
  496.2 137.1 %all-gather.19.cloned.1.call-start = ((), (), s32[]{:S(2)}) async-start(), calls=%async_computation.16 | async-start | bytes 4456448 | tf_op jit(solution)/shard_map/all_gather | solution.py:8
  573.6 143.9 %copy-start.15 = (f32[1,112,128]{2,1,0:T(8,128)S(1)}, f32[1,112,128]{2,1,0:T(8,128)}, u32[]{:S(2)}) copy-start(f32[1,112,128]{2,1,0:T(8,128)} %reduce-scatter.42.cloned.1.call-done) | copy-start | bytes 172036
  594.1 123.4 %reduce-scatter.44.cloned.1.call-start = ((), (), s32[]{:S(2)}) async-start(), calls=%async_computation.25 | async-start | bytes 974848
  640.1 153.3 %reduce-scatter.28.cloned.1.call-start = ((), (), s32[]{:S(2)}) async-start(), calls=%async_computation.17 | async-start | bytes 974848 | tf_op jit(solution)/shard_map/reduce_scatter | solution.py:68
  737.2 192.7 %copy-start.11 = (bf16[112,128]{1,0:T(8,128)(2,1)}, bf16[112,128]{1,0:T(8,128)(2,1)S(1)}, u32[]{:S(2)}) copy-start(bf16[112,128]{1,0:T(8,128)(2,1)S(1)} %get-tuple-element.233) | copy-start | bytes 86020
  738.3 190.4 %all-reduce.9.cloned.1.call-start = ((), (), s32[]{:S(2)}) async-start(), calls=%async_computation.9 | async-start | bytes 524288 | tf_op jit(solution)/shard_map/psum | solution.py:160
  821.5 168.0 %reduce-scatter.30.cloned.1.call-start = ((), (), s32[]{:S(2)}) async-start(), calls=%async_computation.18 | async-start | bytes 974848 | tf_op jit(solution)/shard_map/reduce_scatter | solution.py:68
  929.9 593.5 %copy-start.8 = (bf16[1,112,1792]{2,1,0:T(8,128)(2,1)S(1)}, bf16[1,112,1792]{2,1,0:T(8,128)(2,1)}, u32[]{:S(2)}) copy-start(bf16[1,112,1792]{2,1,0:T(8,128)(2,1)} %param.36) | copy-start | bytes 1204228
  930.9 195.2 %all-reduce.11.cloned.1.call-start = ((), (), s32[]{:S(2)}) async-start(), calls=%async_computation.10 | async-start | bytes 524288 | tf_op jit(solution)/shard_map/psum | solution.py:160
  1019.0 169.2 %reduce-scatter.32.cloned.1.call-start = ((), (), s32[]{:S(2)}) async-start(), calls=%async_computation.19 | async-start | bytes 974848 | tf_op jit(solution)/shard_map/reduce_scatter | solution.py:68
  1129.5 195.0 %all-reduce.13.cloned.1.call-start = ((), (), s32[]{:S(2)}) async-start(), calls=%async_computation.11 | async-start | bytes 524288 | tf_op jit(solution)/shard_map/psum | solution.py:160
  1217.5 168.6 %reduce-scatter.34.cloned.1.call-start = ((), (), s32[]{:S(2)}) async-start(), calls=%async_computation.20 | async-start | bytes 974848 | tf_op jit(solution)/shard_map/reduce_scatter | solution.py:68
  1326.4 196.0 %all-reduce.15.cloned.1.call-start = ((), (), s32[]{:S(2)}) async-start(), calls=%async_computation.12 | async-start | bytes 524288 | tf_op jit(solution)/shard_map/psum | solution.py:160
  1415.5 169.0 %reduce-scatter.36.cloned.1.call-start = ((), (), s32[]{:S(2)}) async-start(), calls=%async_computation.21 | async-start | bytes 974848 | tf_op jit(solution)/shard_map/reduce_scatter | solution.py:68
  (14 other events, 525.0 us)
Sparse Core Ops, SparseCore 0:
  34.3 93.4 all-gather.12
  147.3 77.2 reduce-scatter.37
  245.5 72.8 all-gather.14
  333.7 77.2 reduce-scatter.39
  432.2 52.9 all-gather.16
  496.3 77.2 reduce-scatter.41
  594.2 38.9 all-gather.18
  640.2 77.2 reduce-scatter.43
  738.4 54.9 reduce-scatter.27
  821.6 106.9 all-reduce.8
  931.2 58.3 reduce-scatter.29
  1019.1 106.9 all-reduce.10
  1129.6 58.5 reduce-scatter.31
  1217.6 106.8 all-reduce.12
  1326.9 59.1 reduce-scatter.33
  1415.6 106.7 all-reduce.14
  1526.1 58.3 reduce-scatter.35
